TPU v7x, 256 devices: a whole 4x4x8 slice. The times are simulated.
256 devices in a mesh: seq: 32 (over y, z), dp: 8 (over x, core).
Axes of the slice: x: 4, y: 4, z: 8, core: 2. Of those that a mesh axis runs over, the one named last changes fastest.
Arguments:
- queries: bfloat16 [8, 2048, 16384], P('dp', None, 'seq'), may hold values from -6 to 6
- keys: bfloat16 [8, 2048, 16384], P('dp', None, 'seq'), may hold values from -6 to 6
- values: bfloat16 [8, 2048, 16384], P('dp', None, 'seq'), may hold values from -6 to 6
- random_blocks: int32 [8, 32, 256, 3], P('dp', 'seq'), may hold values from 0 to 255
- global_blocks: int32 [8, 2], P('dp'), may hold values from 0 to 255, as said below
- out_weight: bfloat16 [2048, 2048], P('dp'), may hold values from -0.125 to 0.125
Outputs:
- projected: bfloat16 [8, 16384, 2048], P('dp', 'seq')
Inputs may be any that keep to these rules, and one draw needn't show every extreme that they name: `global_blocks`: the two global blocks of a sequence differ; some sequence has block 0 and some has block 255.
All inputs are finite; a program needn't handle non-finite values.
Results may differ from a plain program's by a relative error of at most 0.01.
Values may be sent and summed in bfloat16 or wider, within the bound.
A program may use at most 128 MiB of HBM per device.

v0:
```python
import math

import jax
import jax.numpy as jnp
from jax import lax
from jax.sharding import PartitionSpec as P

HD = 64
BLK = 64


def candidate_blocks(nblocks, glob, rand_h):
    rows = jnp.arange(nblocks, dtype=jnp.int32)
    window = jnp.stack([rows - 1, rows, rows + 1], axis=1)
    globs = jnp.broadcast_to(glob[None, :], (nblocks, glob.shape[0]))
    cand = jnp.concatenate([window, globs, rand_h], axis=1)
    inside = (cand >= 0) & (cand < nblocks)
    width = cand.shape[1]
    equal = cand[:, :, None] == cand[:, None, :]
    earlier = jnp.arange(width)[None, :] < jnp.arange(width)[:, None]
    repeated = jnp.any(equal & earlier[None, :, :], axis=2)
    return (jnp.clip(cand, 0, nblocks - 1), inside & ~repeated)


def head_attention(q_head, k_head, v_head, rand_h, glob):
    length = q_head.shape[1]
    nblocks = length // BLK
    scale = HD ** (-0.5)
    qb = q_head.reshape(HD, nblocks, BLK)
    kb = k_head.reshape(HD, nblocks, BLK)
    vb = v_head.reshape(HD, nblocks, BLK)
    index, valid = candidate_blocks(nblocks, glob, rand_h)
    group = math.gcd(nblocks, 32)
    turns = nblocks // group

    def one_group(turn):
        first = turn * group
        rows_index = lax.dynamic_slice_in_dim(index, first, group, 0)
        rows_valid = lax.dynamic_slice_in_dim(valid, first, group, 0)
        q_rows = lax.dynamic_slice_in_dim(qb, first, group, 1)
        k_rows = jnp.take(kb, rows_index, axis=1)
        v_rows = jnp.take(vb, rows_index, axis=1)
        scores = (
            jnp.einsum("dnq,dnck->nqck", q_rows, k_rows, preferred_element_type=jnp.float32) * scale
        )
        scores = jnp.where(rows_valid[:, None, :, None], scores, -jnp.inf)
        top = jnp.max(scores, axis=(2, 3), keepdims=True)
        expo = jnp.exp(scores - top)
        probs = (expo / jnp.sum(expo, axis=(2, 3), keepdims=True)).astype(jnp.bfloat16)
        return jnp.einsum(
            "nqck,dnck->dnq", probs, v_rows, preferred_element_type=jnp.float32
        ).astype(jnp.bfloat16)

    parts = lax.map(one_group, jnp.arange(turns, dtype=jnp.int32))
    blocks = jnp.transpose(parts, (1, 0, 2, 3)).reshape(HD, nblocks, BLK)
    qglob = jnp.take(qb, glob, axis=1)
    gscore = jnp.einsum("dgq,dk->gqk", qglob, k_head, preferred_element_type=jnp.float32) * scale
    gtop = jnp.max(gscore, axis=2, keepdims=True)
    gexp = jnp.exp(gscore - gtop)
    gprob = (gexp / jnp.sum(gexp, axis=2, keepdims=True)).astype(jnp.bfloat16)
    full = jnp.einsum("gqk,dk->dgq", gprob, v_head, preferred_element_type=jnp.float32).astype(
        jnp.bfloat16
    )
    blocks = blocks.at[:, glob, :].set(full)
    return blocks.reshape(HD, length)


def local(queries, keys, values, random_blocks, global_blocks, out_weight):
    q_heads, k_heads, v_heads = (
        lax.all_to_all(queries[0], "seq", split_axis=0, concat_axis=1, tiled=True),
        lax.all_to_all(keys[0], "seq", split_axis=0, concat_axis=1, tiled=True),
        lax.all_to_all(values[0], "seq", split_axis=0, concat_axis=1, tiled=True),
    )
    count = q_heads.shape[0] // HD
    length = q_heads.shape[1]
    glob = global_blocks[0]

    def one_head(packed):
        q_head, k_head, v_head, rand_h = packed
        return head_attention(q_head, k_head, v_head, rand_h, glob)

    outputs = lax.map(
        one_head,
        (
            q_heads.reshape(count, HD, length),
            k_heads.reshape(count, HD, length),
            v_heads.reshape(count, HD, length),
            random_blocks[0],
        ),
    )
    attended = lax.all_to_all(
        outputs.reshape(count * HD, length), "seq", split_axis=1, concat_axis=0, tiled=True
    )
    result = lax.dot_general(
        attended,
        lax.all_gather(out_weight, "dp", axis=0, tiled=True),
        (((0,), (0,)), ((), ())),
        preferred_element_type=jnp.float32,
    )
    return result.astype(jnp.bfloat16)[None]


def solution(mesh):
    in_specs = (
        P("dp", None, "seq"),
        P("dp", None, "seq"),
        P("dp", None, "seq"),
        P("dp", "seq", None, None),
        P("dp", None),
        P("dp", None),
    )
    out_specs = P("dp", "seq", None)
    return jax.shard_map(local, mesh=mesh, in_specs=in_specs, out_specs=out_specs, check_vma=False)
```

profile of v0, /device:TPU:40, one launch (start us, length us, event | category | flops | bytes accessed | tf_op | source)
XLA Modules:
  0.0 600.9 jit_solution(8620004116094292782)
XLA Ops:
  6.5 61.7 %all_to_all.67 = bf16[32,64,512]{2,1,0:T(8,128)(2,1)} all-to-all(bf16[32,64,512]{2,1,0:T(8,128)(2,1)} %bitcast.113), channel_id=1, replica_groups=mesh['seq'=32,'dp'=8] {'seq'}, dimensions={0} | all-to-all | bytes 4194304 | tf_op jit(solution)/shard_map/all_to_all | solution.py:70
  68.2 55.7 %all_to_all.68 = bf16[32,64,512]{2,1,0:T(8,128)(2,1)} all-to-all(bf16[32,64,512]{2,1,0:T(8,128)(2,1)S(1)} %bitcast.114), channel_id=1, replica_groups=mesh['seq'=32,'dp'=8] {'seq'}, dimensions={0} | all-to-all | bytes 4194304 | tf_op jit(solution)/shard_map/all_to_all | solution.py:71
  123.9 6.1 %all-to-all-start = ((bf16[32,64,512]{2,1,0:T(8,128)(2,1)}), bf16[32,64,512]{2,1,0:T(8,128)(2,1)}, u32[]{:S(2)}, u32[]{:S(2)}) async-start(bf16[32,64,512]{2,1,0:T(8,128)(2,1)} %bitcast.115), calls=%async_computation | async-start | bytes 4194304 | tf_op jit(solution)/shard_map/all_to_all | solution.py:72
  138.6 7.0 %copy.69 = bf16[64,256,64]{2,0,1:T(8,128)(2,1)} copy(bf16[64,256,64]{2,1,0:T(8,128)(2,1)} %reshape.125) | data formatting | bytes 4194304 | tf_op jit(solution)/shard_map/while/body/eval_jaxpr/while | solution.py:54
  146.8 32.0 %all-to-all-done = bf16[32,64,512]{2,1,0:T(8,128)(2,1)} async-done(((bf16[32,64,512]{2,1,0:T(8,128)(2,1)}), bf16[32,64,512]{2,1,0:T(8,128)(2,1)}, u32[]{:S(2)}, u32[]{:S(2)}) %all-to-all-start) | async-done | bytes 2097184 | tf_op jit(solution)/shard_map/all_to_all | solution.py:72
  178.8 4.2 copy.63
  182.9 6.2 %reshape.124 = bf16[64,256,64]{2,1,0:T(8,128)(2,1)} reshape(bf16[64,32,512]{2,1,0:T(8,128)(2,1)} %copy.63) | data formatting | bytes 4194304 | tf_op jit(solution)/shard_map/while/body/eval_jaxpr/reshape | solution.py:31
  189.1 6.9 %copy.67 = bf16[64,256,64]{2,0,1:T(8,128)(2,1)} copy(bf16[64,256,64]{2,1,0:T(8,128)(2,1)} %reshape.124) | data formatting | bytes 4194304 | tf_op jit(solution)/shard_map/while/body/eval_jaxpr/while | solution.py:54
  199.6 6.8 %copy.70 = bf16[64,256,64]{2,0,1:T(8,128)(2,1)} copy(bf16[64,256,64]{2,1,0:T(8,128)(2,1)} %reshape.126) | data formatting | bytes 4194304 | tf_op jit(solution)/shard_map/while/body/eval_jaxpr/while | solution.py:54
  206.5 292.5 %while.17 = (s32[]{:T(128)}, bf16[8,64,32,64]{3,1,2,0:T(8,128)(2,1)}, s32[8]{0:T(128)S(1)}, s32[256,8]{0,1:T(8,128)S(1)}, bf16[64,256,64]{2,0,1:T(8,128)(2,1)}, ...) while((s32[]{:T(128)}, ...), condition=%wide.region_4.6_spmd, body=%wide.region_1.5_spmd.sunk | while | flops 283245824 | bytes 59837148 | solution.py:54
  208.0 5.2 gather_fusion
  213.3 6.4 %copy.91 = bf16[32,8,64,64]{2,3,1,0:T(8,128)(2,1)} copy(bf16[32,8,64,64]{3,2,1,0:T(8,128)(2,1)} %bitcast.107) | data formatting | bytes 4194304 | tf_op jit(solution)/shard_map/while/body/eval_jaxpr/while/body/eval_jaxpr/jit(_take)/gather | solution.py:41
  219.7 3.8 broadcast_select_fusion.2
  230.2 5.3 gather_fusion.1
  235.5 7.5 %fusion.52 = bf16[8,64,32,64]{3,1,2,0:T(8,128)(2,1)} fusion(bf16[8,64,32,64]{3,1,2,0:T(8,128)(2,1)} %get-tuple-element.193, s32[]{:T(128)} %get-tuple-element.192, f32[32,64,512]{1,2,0} %copy-done, f32[32,64]{1,0:T(8,128)S(1)} %fusion.51, f32[32,64]{1,0:T(8,128)S(1)} %get-tuple-element.179, pred[32,8]{1,0:T(8,128)(4,1)S(1)} %copy.89, ...), kind=kOutput, calls=%fused_computation.19.clone.1 | convolution fusion | flops 140640256 | bytes 8929796 | tf_op jit(solution)/shard_map/while/body/eval_jaxpr/while/body/eval_jaxpr/nqck,dnck->dnq/dot_general | solution.py:50
  244.6 5.2 gather_fusion
  249.8 6.4 %copy.91 = bf16[32,8,64,64]{2,3,1,0:T(8,128)(2,1)} copy(bf16[32,8,64,64]{3,2,1,0:T(8,128)(2,1)} %bitcast.107) | data formatting | bytes 4194304 | tf_op jit(solution)/shard_map/while/body/eval_jaxpr/while/body/eval_jaxpr/jit(_take)/gather | solution.py:41
  266.8 5.3 gather_fusion.1
  272.1 7.5 %fusion.52 = bf16[8,64,32,64]{3,1,2,0:T(8,128)(2,1)} fusion(bf16[8,64,32,64]{3,1,2,0:T(8,128)(2,1)} %get-tuple-element.193, s32[]{:T(128)} %get-tuple-element.192, f32[32,64,512]{1,2,0} %copy-done, f32[32,64]{1,0:T(8,128)S(1)} %fusion.51, f32[32,64]{1,0:T(8,128)S(1)} %get-tuple-element.179, pred[32,8]{1,0:T(8,128)(4,1)S(1)} %copy.89, ...), kind=kOutput, calls=%fused_computation.19.clone.1 | convolution fusion | flops 140640256 | bytes 8929796 | tf_op jit(solution)/shard_map/while/body/eval_jaxpr/while/body/eval_jaxpr/nqck,dnck->dnq/dot_general | solution.py:50
  281.2 5.2 gather_fusion
  286.4 6.4 %copy.91 = bf16[32,8,64,64]{2,3,1,0:T(8,128)(2,1)} copy(bf16[32,8,64,64]{3,2,1,0:T(8,128)(2,1)} %bitcast.107) | data formatting | bytes 4194304 | tf_op jit(solution)/shard_map/while/body/eval_jaxpr/while/body/eval_jaxpr/jit(_take)/gather | solution.py:41
  303.4 5.3 gather_fusion.1
  308.7 7.5 %fusion.52 = bf16[8,64,32,64]{3,1,2,0:T(8,128)(2,1)} fusion(bf16[8,64,32,64]{3,1,2,0:T(8,128)(2,1)} %get-tuple-element.193, s32[]{:T(128)} %get-tuple-element.192, f32[32,64,512]{1,2,0} %copy-done, f32[32,64]{1,0:T(8,128)S(1)} %fusion.51, f32[32,64]{1,0:T(8,128)S(1)} %get-tuple-element.179, pred[32,8]{1,0:T(8,128)(4,1)S(1)} %copy.89, ...), kind=kOutput, calls=%fused_computation.19.clone.1 | convolution fusion | flops 140640256 | bytes 8929796 | tf_op jit(solution)/shard_map/while/body/eval_jaxpr/while/body/eval_jaxpr/nqck,dnck->dnq/dot_general | solution.py:50
  317.7 5.2 gather_fusion
  323.0 6.4 %copy.91 = bf16[32,8,64,64]{2,3,1,0:T(8,128)(2,1)} copy(bf16[32,8,64,64]{3,2,1,0:T(8,128)(2,1)} %bitcast.107) | data formatting | bytes 4194304 | tf_op jit(solution)/shard_map/while/body/eval_jaxpr/while/body/eval_jaxpr/jit(_take)/gather | solution.py:41
  339.9 5.3 gather_fusion.1
  345.2 7.5 %fusion.52 = bf16[8,64,32,64]{3,1,2,0:T(8,128)(2,1)} fusion(bf16[8,64,32,64]{3,1,2,0:T(8,128)(2,1)} %get-tuple-element.193, s32[]{:T(128)} %get-tuple-element.192, f32[32,64,512]{1,2,0} %copy-done, f32[32,64]{1,0:T(8,128)S(1)} %fusion.51, f32[32,64]{1,0:T(8,128)S(1)} %get-tuple-element.179, pred[32,8]{1,0:T(8,128)(4,1)S(1)} %copy.89, ...), kind=kOutput, calls=%fused_computation.19.clone.1 | convolution fusion | flops 140640256 | bytes 8929796 | tf_op jit(solution)/shard_map/while/body/eval_jaxpr/while/body/eval_jaxpr/nqck,dnck->dnq/dot_general | solution.py:50
  354.3 5.2 gather_fusion
  359.5 6.4 %copy.91 = bf16[32,8,64,64]{2,3,1,0:T(8,128)(2,1)} copy(bf16[32,8,64,64]{3,2,1,0:T(8,128)(2,1)} %bitcast.107) | data formatting | bytes 4194304 | tf_op jit(solution)/shard_map/while/body/eval_jaxpr/while/body/eval_jaxpr/jit(_take)/gather | solution.py:41
  376.4 5.3 gather_fusion.1
  381.8 7.5 %fusion.52 = bf16[8,64,32,64]{3,1,2,0:T(8,128)(2,1)} fusion(bf16[8,64,32,64]{3,1,2,0:T(8,128)(2,1)} %get-tuple-element.193, s32[]{:T(128)} %get-tuple-element.192, f32[32,64,512]{1,2,0} %copy-done, f32[32,64]{1,0:T(8,128)S(1)} %fusion.51, f32[32,64]{1,0:T(8,128)S(1)} %get-tuple-element.179, pred[32,8]{1,0:T(8,128)(4,1)S(1)} %copy.89, ...), kind=kOutput, calls=%fused_computation.19.clone.1 | convolution fusion | flops 140640256 | bytes 8929796 | tf_op jit(solution)/shard_map/while/body/eval_jaxpr/while/body/eval_jaxpr/nqck,dnck->dnq/dot_general | solution.py:50
  390.8 5.2 gather_fusion
  396.1 6.4 %copy.91 = bf16[32,8,64,64]{2,3,1,0:T(8,128)(2,1)} copy(bf16[32,8,64,64]{3,2,1,0:T(8,128)(2,1)} %bitcast.107) | data formatting | bytes 4194304 | tf_op jit(solution)/shard_map/while/body/eval_jaxpr/while/body/eval_jaxpr/jit(_take)/gather | solution.py:41
  413.0 5.3 gather_fusion.1
  418.3 7.5 %fusion.52 = bf16[8,64,32,64]{3,1,2,0:T(8,128)(2,1)} fusion(bf16[8,64,32,64]{3,1,2,0:T(8,128)(2,1)} %get-tuple-element.193, s32[]{:T(128)} %get-tuple-element.192, f32[32,64,512]{1,2,0} %copy-done, f32[32,64]{1,0:T(8,128)S(1)} %fusion.51, f32[32,64]{1,0:T(8,128)S(1)} %get-tuple-element.179, pred[32,8]{1,0:T(8,128)(4,1)S(1)} %copy.89, ...), kind=kOutput, calls=%fused_computation.19.clone.1 | convolution fusion | flops 140640256 | bytes 8929796 | tf_op jit(solution)/shard_map/while/body/eval_jaxpr/while/body/eval_jaxpr/nqck,dnck->dnq/dot_general | solution.py:50
  427.4 5.2 gather_fusion
  432.7 6.4 %copy.91 = bf16[32,8,64,64]{2,3,1,0:T(8,128)(2,1)} copy(bf16[32,8,64,64]{3,2,1,0:T(8,128)(2,1)} %bitcast.107) | data formatting | bytes 4194304 | tf_op jit(solution)/shard_map/while/body/eval_jaxpr/while/body/eval_jaxpr/jit(_take)/gather | solution.py:41
  449.6 5.3 gather_fusion.1
  454.9 7.5 %fusion.52 = bf16[8,64,32,64]{3,1,2,0:T(8,128)(2,1)} fusion(bf16[8,64,32,64]{3,1,2,0:T(8,128)(2,1)} %get-tuple-element.193, s32[]{:T(128)} %get-tuple-element.192, f32[32,64,512]{1,2,0} %copy-done, f32[32,64]{1,0:T(8,128)S(1)} %fusion.51, f32[32,64]{1,0:T(8,128)S(1)} %get-tuple-element.179, pred[32,8]{1,0:T(8,128)(4,1)S(1)} %copy.89, ...), kind=kOutput, calls=%fused_computation.19.clone.1 | convolution fusion | flops 140640256 | bytes 8929796 | tf_op jit(solution)/shard_map/while/body/eval_jaxpr/while/body/eval_jaxpr/nqck,dnck->dnq/dot_general | solution.py:50
  464.0 5.2 gather_fusion
  469.2 6.4 %copy.91 = bf16[32,8,64,64]{2,3,1,0:T(8,128)(2,1)} copy(bf16[32,8,64,64]{3,2,1,0:T(8,128)(2,1)} %bitcast.107) | data formatting | bytes 4194304 | tf_op jit(solution)/shard_map/while/body/eval_jaxpr/while/body/eval_jaxpr/jit(_take)/gather | solution.py:41
  486.1 5.3 gather_fusion.1
  491.5 7.5 %fusion.52 = bf16[8,64,32,64]{3,1,2,0:T(8,128)(2,1)} fusion(bf16[8,64,32,64]{3,1,2,0:T(8,128)(2,1)} %get-tuple-element.193, s32[]{:T(128)} %get-tuple-element.192, f32[32,64,512]{1,2,0} %copy-done, f32[32,64]{1,0:T(8,128)S(1)} %fusion.51, f32[32,64]{1,0:T(8,128)S(1)} %get-tuple-element.179, pred[32,8]{1,0:T(8,128)(4,1)S(1)} %copy.89, ...), kind=kOutput, calls=%fused_computation.19.clone.1 | convolution fusion | flops 140640256 | bytes 8929796 | tf_op jit(solution)/shard_map/while/body/eval_jaxpr/while/body/eval_jaxpr/nqck,dnck->dnq/dot_general | solution.py:50
  501.3 4.4 reshape.176
  515.1 6.8 %copy.76 = bf16[64,256,64]{2,1,0:T(8,128)(2,1)} copy(bf16[64,256,64]{2,0,1:T(8,128)(2,1)} %scatter_fusion) | data formatting | bytes 4194304 | tf_op jit(solution)/shard_map/while/body/eval_jaxpr/scatter | solution.py:64
  522.0 5.4 all_to_all.59
  528.5 56.4 %all_to_all.69 = bf16[64,32,512]{2,0,1:T(8,128)(2,1)S(1)} all-to-all(bf16[64,32,512]{2,0,1:T(8,128)(2,1)S(1)} %copy.77), channel_id=1, replica_groups=mesh['seq'=32,'dp'=8] {'seq'}, dimensions={1} | all-to-all | bytes 4194304 | tf_op jit(solution)/shard_map/all_to_all | solution.py:91
  585.0 9.1 %fusion.28 = bf16[1,512,2048]{2,1,0:T(8,128)(2,1)} fusion(bf16[2048,512]{1,0:T(8,128)(2,1)S(1)} %bitcast.116, bf16[2048,2048]{1,0:T(8,128)(2,1)} %all-gather.2.cloned.1.call-done), kind=kOutput, calls=%fused_computation.37 | convolution fusion | flops 4296015872 | bytes 12582912 | tf_op jit(solution)/shard_map/dot_general | solution.py:94
  (158 shorter events, 113.7 us)
Async XLA Ops:
  6.5 61.7 %copy-start.3 = (bf16[1,2048,512]{2,1,0:T(8,128)(2,1)S(1)}, bf16[1,2048,512]{2,1,0:T(8,128)(2,1)}, u32[]{:S(2)}) copy-start(bf16[1,2048,512]{2,1,0:T(8,128)(2,1)} %param.11) | copy-start | bytes 6291460
  68.2 62.5 %copy-start.5 = (s32[1,1,256,3]{2,1,3,0:T(1,128)S(1)}, s32[1,1,256,3]{2,1,3,0:T(1,128)}, u32[]{:S(2)}) copy-start(s32[1,1,256,3]{2,1,3,0:T(1,128)} %param.13) | copy-start | bytes 9220
  68.2 62.5 %copy-start.9 = (s32[1,2]{1,0:T(1,128)S(1)}, s32[1,2]{1,0:T(1,128)}, u32[]{:S(2)}) copy-start(s32[1,2]{1,0:T(1,128)} %param.14) | copy-start | bytes 28
  123.9 54.9 %all-to-all-start = ((bf16[32,64,512]{2,1,0:T(8,128)(2,1)}), bf16[32,64,512]{2,1,0:T(8,128)(2,1)}, u32[]{:S(2)}, u32[]{:S(2)}) async-start(bf16[32,64,512]{2,1,0:T(8,128)(2,1)} %bitcast.115), calls=%async_computation | async-start | bytes 4194304 | tf_op jit(solution)/shard_map/all_to_all | solution.py:72
  130.0 455.0 %all-gather.2.cloned.1.call-start = ((), (), s32[]{:S(2)}) async-start(), calls=%async_computation.4 | async-start | bytes 9437184 | tf_op jit(solution)/shard_map/all_gather | solution.py:96
  130.9 1.3 copy-start.7
  138.6 7.0 %copy-start.1 = (bf16[32,64,512]{2,1,0:T(8,128)(2,1)S(1)}, bf16[32,64,512]{2,1,0:T(8,128)(2,1)}, u32[]{:S(2)}) copy-start(bf16[32,64,512]{2,1,0:T(8,128)(2,1)} %all_to_all.68) | copy-start | bytes 6291460
  227.0 3.2 copy-start
  263.6 3.2 copy-start
  300.1 3.2 copy-start
  336.7 3.2 copy-start
  373.2 3.2 copy-start
  409.8 3.2 copy-start
  446.4 3.2 copy-start
  482.9 3.2 copy-start
  499.0 9.6 %copy-start.6 = (pred[2]{0:T(512)(128)(4,1)S(1)}, pred[2]{0:T(512)(128)(4,1)}, u32[]{:S(2)}) copy-start(pred[2]{0:T(512)(128)(4,1)} %compare_and_fusion.1) | copy-start | bytes 10
  501.3 7.3 %copy-start.2 = (bf16[64,16384,1]{1,0,2:T(8,128)(2,1)S(1)}, bf16[64,16384,1]{1,0,2:T(8,128)(2,1)}, u32[]{:S(2)}) copy-start(bf16[64,16384,1]{1,0,2:T(8,128)(2,1)} %reshape.175) | copy-start | bytes 6291460
  510.0 1.6 copy-start.4
  511.6 1.6 copy-start.8
Sparse Core Ops, SparseCore 0:
  132.7 53.2 all-gather.1
where the time goes:
time: 605 us; the launch traced here: 601 us
  local copies, waits for them, and re-layouts  220 us (36%)
  blocking collectives  174 us (29%)
  matrix products  98.5 us (16%)
  other arithmetic  50.9 us (8%)
  waiting for transfers between devices  32.7 us (5%)
  between operations  13.6 us (2%)
  starting transfers between devices  6.1 us (1%)
    gather x16, local copies, waits for them, and re-layouts, one_group(): k_rows = jnp.take(kb, rows_index, axis=1)  93.1 us
    all_to_all x1, blocking collectives, local(): lax.all_to_all(queries[0], 'seq', split_axis=0, concat_axis=1, tiled=True)  61.7 us
    dot_general x8, matrix products, one_group(): jnp.einsum('nqck,dnck->dnq', probs, v_rows, preferred_element_type=jnp.fl...  60.1 us
    all_to_all x1, blocking collectives, local(): lax.all_to_all(outputs.reshape(count * HD, length), 'seq', split_axis=1,...  56.4 us
    all_to_all x1, blocking collectives, local(): lax.all_to_all(keys[0], 'seq', split_axis=0, concat_axis=1, tiled=True)  55.7 us
    gather x8, local copies, waits for them, and re-layouts, one_group(): v_rows = jnp.take(vb, rows_index, axis=1)  42.6 us
    all_to_all x1, waiting for transfers between devices, local(): lax.all_to_all(values[0], 'seq', split_axis=0, concat_axis=1, tiled=True)  32 us
    select_n x8, other arithmetic, one_group(): k_rows = jnp.take(kb, rows_index, axis=1)  30.6 us
  transfers between devices with their start and end apart: 2, of which 1 were waited for; matrix products, arithmetic and copies ran while one was open for 58% of the time, Pallas kernels for 0%

commit v1 on v0

v1 whole, which is shorter than its diff:
```python
import functools

import jax
import jax.numpy as jnp
from jax import lax
from jax.experimental import pallas as pl
from jax.experimental.pallas import tpu as pltpu
from jax.sharding import PartitionSpec as P

HD = 64
BLK = 64
LANES = 128
CAND = 8
LOG2E = 1.4426950408889634
SCALE = HD ** (-0.5) * LOG2E


def candidate_blocks(nblocks, glob, rand_h):
    rows = jnp.arange(nblocks, dtype=jnp.int32)
    window = jnp.stack([rows - 1, rows, rows + 1], axis=1)
    globs = jnp.broadcast_to(glob[None, :], (nblocks, glob.shape[0]))
    cand = jnp.concatenate([window, globs, rand_h], axis=1)
    inside = (cand >= 0) & (cand < nblocks)
    width = cand.shape[1]
    equal = cand[:, :, None] == cand[:, None, :]
    earlier = jnp.arange(width)[None, :] < jnp.arange(width)[:, None]
    repeated = jnp.any(equal & earlier[None, :, :], axis=2)
    return jnp.clip(cand, 0, nblocks - 1), inside & ~repeated


def rows_of(index, count=BLK):
    return pl.ds(pl.multiple_of(index * count, count), count)


def lane_mask(rows):
    return lax.broadcasted_iota(jnp.int32, (rows, LANES), 1) < HD


def dot_t(a, b):
    return lax.dot_general(a, b, (((1,), (1,)), ((), ())), preferred_element_type=jnp.float32)


def dot_n(a, b):
    return lax.dot_general(a, b, (((1,), (0,)), ((), ())), preferred_element_type=jnp.float32)


def spread(chunk, other):
    return jnp.concatenate([chunk, other], axis=0).T


def sparse_block(block, q_rows, kt, vt, index, bias):
    picks = [rows_of(index[block * CAND + c]) for c in range(CAND)]
    keys = jnp.concatenate([kt[p, :] for p in picks], axis=0)
    scores = dot_t(q_rows, keys) * SCALE
    low = lax.broadcasted_iota(jnp.int32, (1, LANES), 1) < HD
    marks = [
        jnp.where(low, bias[block * CAND + 2 * g], bias[block * CAND + 2 * g + 1])
        for g in range(CAND // 2)
    ]
    scores = scores + jnp.concatenate(marks, axis=1)
    top = jnp.max(scores, axis=1, keepdims=True)
    probs = jnp.exp2(scores - top).astype(jnp.bfloat16)
    vals = jnp.concatenate([vt[p, :] for p in picks], axis=0)
    return dot_n(probs, vals)


def chosen(block, mine, full, glob):
    mine = jnp.where(block == glob[0], full[0:BLK, :], mine)
    return jnp.where(block == glob[1], full[BLK : 2 * BLK, :], mine)


def attend_chunk(chunk, par, out, qt, kt, vt, full, index, bias, glob):
    per = 8
    half = per // 2
    low = lane_mask(BLK)
    for i in range(half):
        first = chunk * per + i + half * par
        second = chunk * per + i + half * (1 - par)
        a = sparse_block(first, qt[rows_of(first), :], kt, vt, index, bias)
        b = sparse_block(second, qt[rows_of(second), :], kt, vt, index, bias)
        a = chosen(first, a, full, glob)
        b = chosen(second, b, full, glob)
        num = jnp.where(low, a, pltpu.roll(b, HD, 1))
        den = jnp.where(low, pltpu.roll(a, HD, 1), b)
        out[i * BLK : (i + 1) * BLK, :] = (num / den).astype(jnp.bfloat16)


def full_blocks(full, qg, kt, vt, held, top):
    turns, _, width = held.shape
    top[...] = jnp.full(top.shape, -jnp.inf, jnp.float32)

    def scores(t, c):
        s = dot_t(qg, kt[rows_of(t, width), :]) * SCALE
        held[t] = s
        best = top[...]
        for g in range(width // LANES):
            best = jnp.maximum(best, s[:, g * LANES : (g + 1) * LANES])
        top[...] = best
        return c

    lax.fori_loop(0, turns, scores, 0)
    best = jnp.max(top[...], axis=1, keepdims=True)
    full[...] = jnp.zeros(full.shape, jnp.float32)

    def values(t, c):
        p = jnp.exp2(held[t] - best).astype(jnp.bfloat16)
        full[...] += dot_n(p, vt[rows_of(t, width), :])
        return c

    lax.fori_loop(0, turns, values, 0)


def attention_kernel(index, bias, glob, q, k, v, out, qt, kt, vt, full, held, top):
    devices, _, width = q.shape
    me = lax.axis_index("seq")
    par = lax.rem(me, 2)

    def turn(s, c):
        rows = rows_of(s, width)
        qt[rows, :] = spread(q[s], q[s])
        kt[rows, :] = spread(k[s], jnp.zeros_like(k[s]))
        vt[rows, :] = spread(v[s], jnp.ones_like(v[s]))
        return c

    lax.fori_loop(0, devices, turn, 0)
    qg = jnp.concatenate([qt[rows_of(glob[0]), :], qt[rows_of(glob[1]), :]], axis=0)
    full_blocks(full, qg, kt, vt, held, top)

    def chunk(s, c):
        attend_chunk(s, par, out.at[s], qt, kt, vt, full, index, bias, glob)
        return c

    lax.fori_loop(0, devices, chunk, 0)


def project_kernel(heads, w, out, total):
    devices, half, _ = heads.shape
    low = lane_mask(half)
    total[...] = jnp.zeros(total.shape, jnp.float32)

    def group(g, c):
        lo, hi, w_lo, w_hi = [], [], [], []
        for p in range(2):
            a, b = heads[4 * g + 2 * p], heads[4 * g + 2 * p + 1]
            lo.append(jnp.where(low, a, b))
            hi.append(jnp.where(low, b, a))
            w_a, w_b = w[rows_of(4 * g + 2 * p), :], w[rows_of(4 * g + 2 * p + 1), :]
            w_lo += [w_a, w_b]
            w_hi += [w_b, w_a]
        total[0:half, :] += dot_n(jnp.concatenate(lo, axis=1), jnp.concatenate(w_lo, axis=0))
        total[half:, :] += dot_n(jnp.concatenate(hi, axis=1), jnp.concatenate(w_hi, axis=0))
        return c

    lax.fori_loop(0, devices // 4, group, 0)
    out[...] = total[...].astype(jnp.bfloat16)


VM = pl.BlockSpec(memory_space=pltpu.VMEM)
SM = pl.BlockSpec(memory_space=pltpu.SMEM)


def attention(index, bias, glob, q, k, v):
    devices, _, width = q.shape
    length = devices * width
    return pl.pallas_call(
        attention_kernel,
        out_shape=jax.ShapeDtypeStruct((devices, width // 2, LANES), jnp.bfloat16),
        in_specs=[SM, SM, SM, VM, VM, VM],
        out_specs=VM,
        scratch_shapes=[
            pltpu.VMEM((length, LANES), jnp.bfloat16),
            pltpu.VMEM((length, LANES), jnp.bfloat16),
            pltpu.VMEM((length, LANES), jnp.bfloat16),
            pltpu.VMEM((2 * BLK, LANES), jnp.float32),
            pltpu.VMEM((devices, 2 * BLK, width), jnp.float32),
            pltpu.VMEM((2 * BLK, LANES), jnp.float32),
        ],
        compiler_params=pltpu.CompilerParams(vmem_limit_bytes=60 << 20),
    )(index, bias, glob, q, k, v)


def project(heads, w):
    devices, half, _ = heads.shape
    return pl.pallas_call(
        project_kernel,
        out_shape=jax.ShapeDtypeStruct((2 * half, w.shape[1]), jnp.bfloat16),
        in_specs=[VM, VM],
        out_specs=VM,
        scratch_shapes=[pltpu.VMEM((2 * half, w.shape[1]), jnp.float32)],
        compiler_params=pltpu.CompilerParams(vmem_limit_bytes=60 << 20),
    )(heads, w)


def local(queries, keys, values, random_blocks, global_blocks, out_weight):
    glob = global_blocks[0]
    width = queries.shape[2]

    def exchange(x):
        return lax.all_to_all(x, "seq", split_axis=0, concat_axis=0, tiled=True)

    k, v, q = (
        exchange(x[0].reshape(-1, HD, width)) for x in (keys, values, queries)
    )
    index, valid = candidate_blocks(random_blocks.shape[2], glob, random_blocks[0, 0])
    bias = jnp.where(valid, 0.0, -jnp.inf).astype(jnp.float32)
    heads = attention(index.reshape(-1), bias.reshape(-1), glob, q, k, v)
    heads = exchange(heads)
    w = lax.all_gather(out_weight, "dp", axis=0, tiled=True)
    return project(heads, w)[None]


def solution(mesh):
    in_specs = (
        P("dp", None, "seq"),
        P("dp", None, "seq"),
        P("dp", None, "seq"),
        P("dp", "seq", None, None),
        P("dp", None),
        P("dp", None),
    )
    out_specs = P("dp", "seq", None)
    return jax.shard_map(local, mesh=mesh, in_specs=in_specs, out_specs=out_specs, check_vma=False)
```

time: 605 us -> 350 us (0.58)
  local copies, waits for them, and re-layouts: 220 us -> 3.1 us
  Pallas kernels: 0 us -> 104 us
  matrix products: 98.5 us -> 0 us
  waiting for transfers between devices: 32.7 us -> 95.8 us
  blocking collectives: 174 us -> 114 us
  other arithmetic: 50.9 us -> 0.12 us
  starting transfers between devices: 6.1 us -> 17.4 us
    gather x25 -> x0, local copies, waits for them, and re-layouts: 139 us -> none  [the longest x16 93.1 us: one_group(): k_rows = jnp.take(kb, rows_index, axis=1)]
    pallas_call x0 -> x2, Pallas kernels: none -> 104 us  [the longest x1 92.7 us: attention(): pl.pallas_call(attention_kernel, out_shape=jax.ShapeDtypeStruct((devices,...]
    dot_general x11 -> x0, matrix products: 72.2 us -> none  [the longest x8 60.1 us: one_group(): jnp.einsum('nqck,dnck->dnq', probs, v_rows, preferred_element_type=jnp.fl...]
    all_to_all x1 -> x2, waiting for transfers between devices: 32 us -> 95.1 us  [exchange(): return lax.all_to_all(x, 'seq', split_axis=0, concat_axis=0, tiled=True)]
    all_to_all x3 -> x2, blocking collectives: 174 us -> 114 us  [exchange(): return lax.all_to_all(x, 'seq', split_axis=0, concat_axis=0, tiled=True)]
    select_n x17 -> x1, other arithmetic: 30.6 us -> 0.01 us  [local(): bias = jnp.where(valid, 0.0, -jnp.inf).astype(jnp.float32)]
    while x19 -> x0, local copies, waits for them, and re-layouts: 29.1 us -> none  [the longest x3 20.7 us: head_attention(): parts = lax.map(one_group, jnp.arange(turns, dtype=jnp.int32))]
    while x8 -> x0, matrix products: 26.4 us -> none
  transfers between devices with their start and end apart: 2 -> 3, of which waited for: 1 -> 2; matrix products, arithmetic and copies ran while one was open for 58% -> 1% of each run, Pallas kernels for 0% -> 27%
where the time goes in v1:
time: 350 us; the launch traced here: 348 us
  blocking collectives  114 us (33%)
  Pallas kernels  104 us (30%)
  waiting for transfers between devices  95.8 us (27%)
  starting transfers between devices  17.4 us (5%)
  between operations  13.5 us (4%)
    all_to_all x2, blocking collectives, exchange(): return lax.all_to_all(x, 'seq', split_axis=0, concat_axis=0, tiled=True)  114 us
    all_to_all x2, waiting for transfers between devices, exchange(): return lax.all_to_all(x, 'seq', split_axis=0, concat_axis=0, tiled=True)  95.1 us
    pallas_call x1, Pallas kernels, attention(): pl.pallas_call(attention_kernel, out_shape=jax.ShapeDtypeStruct((devices,...  92.7 us
    all_to_all x2, starting transfers between devices, exchange(): return lax.all_to_all(x, 'seq', split_axis=0, concat_axis=0, tiled=True)  17.4 us
    pallas_call x1, Pallas kernels, project(): pl.pallas_call(project_kernel, out_shape=jax.ShapeDtypeStruct((2 * half,...  11.6 us
  transfers between devices with their start and end apart: 3, of which 2 were waited for; matrix products, arithmetic and copies ran while one was open for 1% of the time, Pallas kernels for 27%

profile of v1, /device:TPU:40, one launch (start us, length us, event | category | flops | bytes accessed | tf_op | source)
XLA Modules:
  0.0 348.0 jit_solution(16741364434244183396)
XLA Ops:
  6.5 11.2 %all-to-all-start = ((bf16[32,64,512]{2,1,0:T(8,128)(2,1)}), bf16[32,64,512]{2,1,0:T(8,128)(2,1)S(1)}, u32[]{:S(2)}, u32[]{:S(2)}) async-start(bf16[32,64,512]{2,1,0:T(8,128)(2,1)} %bitcast.8), calls=%async_computation | async-start | bytes 4194304 | tf_op jit(solution)/shard_map/all_to_all | solution.py:199
  17.8 0.0 all-gather.2.cloned.1.call-start
  17.8 0.7 all-gather.2.cloned.1.call-update
  18.5 48.3 %all-to-all-done.q = bf16[32,64,512]{2,1,0:T(8,128)(2,1)S(1)} async-done(((bf16[32,64,512]{2,1,0:T(8,128)(2,1)}), bf16[32,64,512]{2,1,0:T(8,128)(2,1)S(1)}, u32[]{:S(2)}, u32[]{:S(2)}) %all-to-all-start) | async-done | bytes 2097184 | tf_op jit(solution)/shard_map/all_to_all | solution.py:199
  66.8 0.0 copy-start
  66.8 57.1 %all_to_all.20.k = bf16[32,64,512]{2,1,0:T(8,128)(2,1)} all-to-all(bf16[32,64,512]{2,1,0:T(8,128)(2,1)} %bitcast.9), channel_id=1, replica_groups=mesh['seq'=32,'dp'=8] {'seq'}, dimensions={0} | all-to-all | bytes 4194304 | tf_op jit(solution)/shard_map/all_to_all | solution.py:199
  124.0 0.0 copy-done
  124.0 0.0 copy-start.2
  124.0 0.0 copy-start.3
  124.0 6.1 %all-to-all-start.2 = ((bf16[32,64,512]{2,1,0:T(8,128)(2,1)}), bf16[32,64,512]{2,1,0:T(8,128)(2,1)S(1)}, u32[]{:S(2)}, u32[]{:S(2)}) async-start(bf16[32,64,512]{2,1,0:T(8,128)(2,1)} %bitcast.10), calls=%async_computation.2 | async-start | bytes 4194304 | tf_op jit(solution)/shard_map/all_to_all | solution.py:199
  130.1 0.0 copy-done.2
  130.2 0.0 copy-done.3
  130.2 0.1 broadcast_in_dim.24
  130.3 0.1 and_reduce_fusion
  130.4 0.1 copy.14
  130.5 0.7 select_n.9.bias
  131.2 0.1 copy.13
  131.4 0.7 min.12.index
  132.1 46.8 %all-to-all-done.2.v = bf16[32,64,512]{2,1,0:T(8,128)(2,1)S(1)} async-done(((bf16[32,64,512]{2,1,0:T(8,128)(2,1)}), bf16[32,64,512]{2,1,0:T(8,128)(2,1)S(1)}, u32[]{:S(2)}, u32[]{:S(2)}) %all-to-all-start.2) | async-done | bytes 2097184 | tf_op jit(solution)/shard_map/all_to_all | solution.py:199
  178.9 0.0 copy-start.1
  178.9 1.3 copy-done.1
  180.2 92.7 %shard_map.64 = bf16[32,256,128]{2,1,0:T(8,128)(2,1)} custom-call(s32[2048]{0:T(1024)} %min.12.index, f32[2048]{0:T(1024)} %select_n.9.bias, s32[2]{0:T(128)} %bitcast.12, bf16[32,64,512]{2,1,0:T(8,128)(2,1)} %copy-done, bf16[32,64,512]{2,1,0:T(8,128)(2,1)} %all_to_all.20.k, bf16[32,64,512]{2,1,0:T(8,128)(2,1)} %copy-done.1), custom_call_target="tpu_custom_call" | custom-call | tf_op jit(solution)/shard_map/pallas_call | solution.py:165
  272.9 56.7 %all_to_all.21.heads = bf16[32,256,128]{2,1,0:T(8,128)(2,1)} all-to-all(bf16[32,256,128]{2,1,0:T(8,128)(2,1)} %shard_map.64), channel_id=1, replica_groups=mesh['seq'=32,'dp'=8] {'seq'}, dimensions={0} | all-to-all | bytes 4194304 | tf_op jit(solution)/shard_map/all_to_all | solution.py:199
  329.6 0.0 all-gather.2.cloned.1.call-done.w
  329.6 11.6 %shard_map.65 = bf16[512,2048]{1,0:T(8,128)(2,1)} custom-call(bf16[32,256,128]{2,1,0:T(8,128)(2,1)} %all_to_all.21.heads, bf16[2048,2048]{1,0:T(8,128)(2,1)} %all-gather.2.cloned.1.call-done.w), custom_call_target="tpu_custom_call" | custom-call | tf_op jit(solution)/shard_map/pallas_call | solution.py:184
  (7 shorter events, 0.1 us)
Async XLA Ops:
  6.5 60.3 %all-to-all-start = ((bf16[32,64,512]{2,1,0:T(8,128)(2,1)}), bf16[32,64,512]{2,1,0:T(8,128)(2,1)S(1)}, u32[]{:S(2)}, u32[]{:S(2)}) async-start(bf16[32,64,512]{2,1,0:T(8,128)(2,1)} %bitcast.8), calls=%async_computation | async-start | bytes 4194304 | tf_op jit(solution)/shard_map/all_to_all | solution.py:199
  17.8 311.8 %all-gather.2.cloned.1.call-start = ((), (), s32[]{:S(2)}) async-start(), calls=%async_computation.4 | async-start | bytes 9437184 | tf_op jit(solution)/shard_map/all_gather | solution.py:208
  66.8 57.1 %copy-start = (bf16[32,64,512]{2,1,0:T(8,128)(2,1)}, bf16[32,64,512]{2,1,0:T(8,128)(2,1)S(1)}, u32[]{:S(2)}) copy-start(bf16[32,64,512]{2,1,0:T(8,128)(2,1)S(1)} %all-to-all-done.q) | copy-start | bytes 6291460
  124.0 6.1 %copy-start.2 = (s32[1,1,256,3]{2,1,3,0:T(1,128)S(1)}, s32[1,1,256,3]{2,1,3,0:T(1,128)}, u32[]{:S(2)}) copy-start(s32[1,1,256,3]{2,1,3,0:T(1,128)} %param.9) | copy-start | bytes 9220
  124.0 6.2 %copy-start.3 = (s32[1,2]{1,0:T(1,128)S(1)}, s32[1,2]{1,0:T(1,128)}, u32[]{:S(2)}) copy-start(s32[1,2]{1,0:T(1,128)} %param.10) | copy-start | bytes 28
  124.0 54.9 %all-to-all-start.2 = ((bf16[32,64,512]{2,1,0:T(8,128)(2,1)}), bf16[32,64,512]{2,1,0:T(8,128)(2,1)S(1)}, u32[]{:S(2)}, u32[]{:S(2)}) async-start(bf16[32,64,512]{2,1,0:T(8,128)(2,1)} %bitcast.10), calls=%async_computation.2 | async-start | bytes 4194304 | tf_op jit(solution)/shard_map/all_to_all | solution.py:199
  178.9 1.3 copy-start.1
Sparse Core Ops, SparseCore 0:
  20.5 53.2 all-gather.1

commit v2 on v0

v2 whole, which is shorter than its diff:
```python
import functools

import jax
import jax.numpy as jnp
from jax import lax
from jax.experimental import pallas as pl
from jax.experimental.pallas import tpu as pltpu
from jax.sharding import PartitionSpec as P

HD = 64
BLK = 64
LANES = 128
CAND = 8
QUAD = 4 * BLK
SCALE = HD ** (-0.5) * 1.4426950408889634
MESH = pl.DeviceIdType.MESH


def candidate_blocks(nblocks, glob, rand_h):
    rows = jnp.arange(nblocks, dtype=jnp.int32)
    window = jnp.stack([rows - 1, rows, rows + 1], axis=1)
    globs = jnp.broadcast_to(glob[None, :], (nblocks, glob.shape[0]))
    cand = jnp.concatenate([window, globs, rand_h], axis=1)
    inside = (cand >= 0) & (cand < nblocks)
    width = cand.shape[1]
    equal = cand[:, :, None] == cand[:, None, :]
    earlier = jnp.arange(width)[None, :] < jnp.arange(width)[:, None]
    repeated = jnp.any(equal & earlier[None, :, :], axis=2)
    return jnp.clip(cand, 0, nblocks - 1), inside & ~repeated


def dot(a, b):
    return lax.dot_general(a, b, (((1,), (0,)), ((), ())), preferred_element_type=jnp.float32)


def lane(shape):
    return lax.broadcasted_iota(jnp.int32, shape, len(shape) - 1)


def low_half(rows):
    return lane((rows, LANES)) < BLK


def swap(x):
    return jnp.concatenate([x[:, BLK:], x[:, :BLK]], axis=1)


def take_query(s, q, qg, glob):
    at = lane((HD, LANES))
    want = jnp.where(at < BLK, glob[0], glob[1])
    kept = qg[...]
    for i in range(q.shape[1] // LANES):
        x = q[:, i * LANES : (i + 1) * LANES]
        first = s * (q.shape[1] // BLK) + 2 * i
        here = first + jnp.where(at < BLK, 0, 1)
        there = first + jnp.where(at < BLK, 1, 0)
        kept = jnp.where(here == want, x, jnp.where(there == want, swap(x), kept))
    qg[...] = kept


def take_key(s, k, kd, qg, held, top):
    per = k.shape[1] // BLK
    tokens = jnp.concatenate([k[...], k[...]], axis=0).T
    for i in range(per):
        kd[s * per + i] = tokens[i * BLK : (i + 1) * BLK, :]
    half = k.shape[1] // 2
    pairs = jnp.where(low_half(half), tokens[:half, :], tokens[half:, :])
    g = qg[...]
    zero = jnp.zeros_like(g)
    weights = jnp.concatenate(
        [jnp.concatenate([g, zero], axis=1), jnp.concatenate([zero, g], axis=1)], axis=0
    )
    scores = dot(pairs, weights) * SCALE
    held[s] = scores
    best = top[...]
    for r in range(half // 8):
        best = jnp.maximum(best, scores[r * 8 : (r + 1) * 8, :])
    top[...] = best


def top_of(top):
    best = jnp.max(top[...], axis=0, keepdims=True)
    best = jnp.maximum(best[:, :LANES], best[:, LANES:])
    return jnp.concatenate([best, best], axis=1)


def take_value(s, v, vd, held, top, full):
    per = v.shape[1] // BLK
    low = low_half(HD)
    for i in range(per // 2):
        x = v[:, i * LANES : (i + 1) * LANES]
        y = swap(x)
        vd[s * per + 2 * i] = jnp.where(low, x, y)
        vd[s * per + 2 * i + 1] = jnp.where(low, y, x)
    half = v.shape[1] // 2
    probs = jnp.exp2(held[s] - top_of(top)).astype(jnp.bfloat16)
    ones = jnp.ones((16, half), jnp.bfloat16)
    lhs = jnp.concatenate([v[:, :half], v[:, half:], ones], axis=0)
    full[...] += dot(lhs, probs)


def finish_full(full, fd):
    num = full[:HD, :LANES] + full[HD : 2 * HD, LANES:]
    row = full[2 * HD : 2 * HD + 1, :]
    out = (num / (row[:, :LANES] + row[:, LANES:])).astype(jnp.bfloat16)
    low = low_half(HD)
    other = swap(out)
    fd[0] = jnp.where(low, out, other)
    fd[1] = jnp.where(low, other, out)


def attend_quad(quad, qq, kd, vd, fd, index, bias, glob):
    low = low_half(BLK)
    base = quad * (4 * CAND)
    at = lane((HD, QUAD)) // BLK
    zero = jnp.zeros_like(qq)
    weights = jnp.concatenate([jnp.where(at == a, qq, zero) for a in range(4)], axis=0)
    picks = [[index[base + a * CAND + c] for c in range(CAND)] for a in range(4)]
    keys = []
    for c in range(CAND):
        k = [kd[picks[a][c]] for a in range(4)]
        keys.append(
            jnp.concatenate([jnp.where(low, k[0], k[1]), jnp.where(low, k[2], k[3])], axis=1)
        )
    scores = dot(jnp.concatenate(keys, axis=0), weights) * SCALE
    marks = bias[quad]
    scores = jnp.concatenate(
        [scores[c * BLK : (c + 1) * BLK, :] + marks[c : c + 1, :] for c in range(CAND)], axis=0
    )
    top = jnp.max(scores, axis=0, keepdims=True)
    probs = jnp.exp2(scores - top).astype(jnp.bfloat16)
    vals = []
    for a in range(4):
        v = [vd[picks[a][c]] for c in range(CAND)]
        vals.append(
            jnp.concatenate(
                [jnp.where(low, v[2 * g], v[2 * g + 1]) for g in range(CAND // 2)], axis=1
            )
        )
    vals.append(jnp.ones((16, CAND * BLK), jnp.bfloat16))
    got = dot(jnp.concatenate(vals, axis=0), probs)
    num = jnp.concatenate(
        [
            jnp.where(low, got[0:64, :LANES], got[64:128, :LANES]),
            jnp.where(low, got[128:192, LANES:], got[192:256, LANES:]),
        ],
        axis=1,
    )
    out = (num / got[256:257, :]).astype(jnp.bfloat16)
    here = quad * 4 + at
    for g in range(2):
        f = fd[g]
        out = jnp.where(here == glob[g], jnp.concatenate([f, f], axis=1), out)
    return out


def tables(glob, rand_h):
    index, valid = candidate_blocks(rand_h.shape[0], glob, rand_h)
    marks = jnp.where(valid, 0.0, -jnp.inf).astype(jnp.float32)
    marks = marks.reshape(-1, 4, CAND).transpose(0, 2, 1)
    return index.reshape(-1), jnp.repeat(marks, BLK, axis=2)


VM = pl.BlockSpec(memory_space=pltpu.VMEM)
SM = pl.BlockSpec(memory_space=pltpu.SMEM)
HB = pl.BlockSpec(memory_space=pl.ANY)

NY = 4
NZ = 8
GROUP = 8


def offset(i):
    a = i // NY
    dz = NZ // 2 + ((a + 1) // 2) * (1 - 2 * lax.rem(a, 2))
    return lax.rem(i + 1, NY), dz


def target(me, i):
    dy, dz = offset(i)
    return lax.rem(me // NZ + dy, NY) * NZ + lax.rem(lax.rem(me, NZ) + dz, NZ)


def source(me, i):
    dy, dz = offset(i)
    return lax.rem(me // NZ + NY - dy, NY) * NZ + lax.rem(lax.rem(me, NZ) + NZ - dz, NZ)


def loop(first, last, f):
    def body(i, c):
        f(i)
        return c

    lax.fori_loop(first, last, body, 0)


def layer_kernel(
    index, glob, bias, q, k, v, w, out,
    qr, kr, vr, kd, vd, fd, qg, held, top, full, ob, att, wr, lhs, total,
    sent, got, w_sent, w_got, own,
):
    devices, _, width = qr.shape
    parts = wr.shape[0] // w.shape[0]
    me = lax.axis_index("seq")
    dp = lax.axis_index("dp")
    barrier = pltpu.get_barrier_semaphore()

    def hello(axis, size, at):
        def one(i):
            pl.semaphore_signal(
                barrier, 1, device_id={axis: lax.rem(at + i, size)}, device_id_type=MESH
            )

        loop(1, size, one)

    hello("seq", devices, me)
    hello("dp", parts, dp)
    pl.semaphore_wait(barrier, devices - 1 + parts - 1)

    def remote(t, i, src, dst, to, from_):
        return pltpu.make_async_remote_copy(
            src_ref=src,
            dst_ref=dst,
            send_sem=sent.at[t, i],
            recv_sem=got.at[t, from_],
            device_id={"seq": to},
            device_id_type=MESH,
        )

    pairs = [(q, qr), (k, kr), (v, vr)]

    def send(t, i):
        to = target(me, i)
        return remote(t, i, pairs[t][0].at[to], pairs[t][1].at[me], to, me)

    def arrive(t, i):
        s = source(me, i)
        remote(t, i, pairs[t][0].at[s], pairs[t][1].at[s], s, s).wait_recv()

    def send_w(i, at):
        to = lax.rem(dp + i, parts)
        return pltpu.make_async_remote_copy(
            src_ref=w,
            dst_ref=wr.at[pl.ds(at * w.shape[0], w.shape[0])],
            send_sem=w_sent.at[i],
            recv_sem=w_got.at[i],
            device_id={"dp": to},
            device_id_type=MESH,
        )

    copies = [pltpu.make_async_copy(a.at[me], b.at[me], own.at[t]) for t, (a, b) in enumerate(pairs)]
    copies.append(
        pltpu.make_async_copy(w, wr.at[pl.ds(dp * w.shape[0], w.shape[0])], own.at[3])
    )
    for t in range(3):
        loop(0, devices - 1, lambda i: send(t, i).start())
        copies[t].start()
        if t == 0:
            loop(1, parts, lambda i: send_w(i, dp).start())
            copies[3].start()

    qg[...] = jnp.zeros(qg.shape, qg.dtype)
    top[...] = jnp.full(top.shape, -jnp.inf, jnp.float32)
    full[...] = jnp.zeros(full.shape, jnp.float32)

    def take(t, f):
        copies[t].wait()

        def one(i):
            @pl.when(i < devices - 1)
            def _():
                arrive(t, i)

            f(source(me, i))

        loop(0, devices, one)

    take(0, lambda s: take_query(s, qr.at[s], qg, glob))
    take(1, lambda s: take_key(s, kr.at[s], kd, qg, held, top))
    take(2, lambda s: take_value(s, vr.at[s], vd, held, top, full))
    finish_full(full, fd)

    def send_o(i):
        to = target(me, i)
        return remote(3, i, ob.at[i], att.at[me], to, me)

    def project(g, last):
        rows = []
        heads = [source(me, g * GROUP + j) for j in range(GROUP)]
        for j in range(GROUP):
            s = heads[j]
            if not (last and j == GROUP - 1):
                remote(3, g * GROUP + j, ob.at[j], att.at[s], s, s).wait_recv()
            rows.append(att[s])
        lhs[...] = jnp.concatenate(rows, axis=0).T

        def tile(n):
            cols = pl.ds(pl.multiple_of(n * QUAD, QUAD), QUAD)
            part = dot(lhs[...], jnp.concatenate([wr[h, :, cols] for h in heads], axis=0))
            if last:
                out[:, cols] = (total[:, cols] + part).astype(jnp.bfloat16)
            else:
                total[:, cols] += part

        loop(0, out.shape[1] // QUAD, tile)

    total[...] = jnp.zeros(total.shape, jnp.float32)
    copies[3].wait()
    loop(1, parts, lambda i: send_w(i, lax.rem(dp + parts - i, parts)).wait_recv())

    def group(g):
        def one(j):
            i = g * GROUP + j
            d = target(me, i)
            for h in range(width // QUAD):
                cols = slice(h * QUAD, (h + 1) * QUAD)
                ob[i, :, cols] = attend_quad(
                    d * (width // QUAD) + h, qr[d, :, cols], kd, vd, fd, index, bias, glob
                )

            @pl.when(i > 0)
            def _():
                send_o(i - 1).start()

        loop(0, GROUP, one)

        @pl.when(g > 0)
        def _():
            project(g - 1, False)

    groups = devices // GROUP
    loop(0, groups, group)
    att[me] = ob[devices - 1]
    project(groups - 1, True)

    for t in range(3):
        loop(0, devices - 1, lambda i: send(t, i).wait_send())
    loop(0, devices - 1, lambda i: send_o(i).wait_send())
    loop(1, parts, lambda i: send_w(i, dp).wait_send())


def layer(index, glob, bias, q, k, v, w, parts):
    devices, _, width = q.shape
    blocks = devices * width // BLK
    columns = w.shape[2]
    bf = jnp.bfloat16
    dma = pltpu.SemaphoreType.DMA
    return pl.pallas_call(
        layer_kernel,
        out_shape=jax.ShapeDtypeStruct((width, columns), bf),
        in_specs=[SM, SM, VM, HB, HB, HB, HB],
        out_specs=VM,
        scratch_shapes=[
            pltpu.VMEM((devices, HD, width), bf),
            pltpu.VMEM((devices, HD, width), bf),
            pltpu.VMEM((devices, HD, width), bf),
            pltpu.VMEM((blocks, BLK, LANES), bf),
            pltpu.VMEM((blocks, HD, LANES), bf),
            pltpu.VMEM((2, HD, LANES), bf),
            pltpu.VMEM((HD, LANES), bf),
            pltpu.VMEM((devices, width // 2, 2 * LANES), jnp.float32),
            pltpu.VMEM((8, 2 * LANES), jnp.float32),
            pltpu.VMEM((2 * HD + 16, 2 * LANES), jnp.float32),
            pltpu.VMEM((devices, HD, width), bf),
            pltpu.VMEM((devices, HD, width), bf),
            pltpu.VMEM((w.shape[0] * parts, HD, columns), bf),
            pltpu.VMEM((width, GROUP * HD), bf),
            pltpu.VMEM((width, columns), jnp.float32),
            dma((4, devices)),
            dma((4, devices)),
            dma((parts,)),
            dma((parts,)),
            dma((4,)),
        ],
        compiler_params=pltpu.CompilerParams(
            collective_id=0, has_side_effects=True, vmem_limit_bytes=60 << 20
        ),
    )(index, glob, bias, q, k, v, w)


def local(queries, keys, values, random_blocks, global_blocks, out_weight):
    glob = global_blocks[0]
    width = queries.shape[2]
    index, bias = tables(glob, random_blocks[0, 0])
    q, k, v = (x[0].reshape(-1, HD, width) for x in (queries, keys, values))
    w = out_weight.reshape(-1, HD, out_weight.shape[1])
    parts = lax.axis_size("dp")
    return layer(index, glob, bias, q, k, v, w, parts)[None]


def solution(mesh):
    in_specs = (
        P("dp", None, "seq"),
        P("dp", None, "seq"),
        P("dp", None, "seq"),
        P("dp", "seq", None, None),
        P("dp", None),
        P("dp", None),
    )
    out_specs = P("dp", "seq", None)
    return jax.shard_map(local, mesh=mesh, in_specs=in_specs, out_specs=out_specs, check_vma=False)
```

time: 605 us -> 228 us (0.38)
  Pallas kernels: 0 us -> 217 us
  local copies, waits for them, and re-layouts: 220 us -> 8.87 us
  blocking collectives: 174 us -> 0 us
  matrix products: 98.5 us -> 0 us
  other arithmetic: 50.9 us -> 0.85 us
  waiting for transfers between devices: 32.7 us -> 0 us
  between operations: 13.6 us -> 0.08 us
  starting transfers between devices: 6.1 us -> 0 us
    pallas_call x0 -> x1, Pallas kernels: none -> 217 us  [layer(): pl.pallas_call(layer_kernel, out_shape=jax.ShapeDtypeStruct((width, colum...]
    all_to_all x3 -> x0, blocking collectives: 174 us -> none  [the longest x1 61.7 us: local(): lax.all_to_all(queries[0], 'seq', split_axis=0, concat_axis=1, tiled=True)]
    gather x25 -> x0, local copies, waits for them, and re-layouts: 139 us -> none  [the longest x16 93.1 us: one_group(): k_rows = jnp.take(kb, rows_index, axis=1)]
    dot_general x11 -> x0, matrix products: 72.2 us -> none  [the longest x8 60.1 us: one_group(): jnp.einsum('nqck,dnck->dnq', probs, v_rows, preferred_element_type=jnp.fl...]
    all_to_all x1 -> x0, waiting for transfers between devices: 32 us -> none  [local(): lax.all_to_all(values[0], 'seq', split_axis=0, concat_axis=1, tiled=True)]
    select_n x17 -> x0, other arithmetic: 30.6 us -> none  [the longest x8 30.6 us: one_group(): k_rows = jnp.take(kb, rows_index, axis=1)]
    while x19 -> x0, local copies, waits for them, and re-layouts: 29.1 us -> none  [the longest x3 20.7 us: head_attention(): parts = lax.map(one_group, jnp.arange(turns, dtype=jnp.int32))]
    while x8 -> x0, matrix products: 26.4 us -> none
  transfers between devices with their start and end apart: 2 -> 0, of which waited for: 1 -> 0; matrix products, arithmetic and copies ran while one was open for 58% -> 0% of each run, Pallas kernels for 0% -> 0%
where the time goes in v2:
time: 228 us; the launch traced here: 227 us
  Pallas kernels  217 us (95%)
  local copies, waits for them, and re-layouts  8.87 us (4%)
    pallas_call x1, Pallas kernels, layer(): pl.pallas_call(layer_kernel, out_shape=jax.ShapeDtypeStruct((width, colum...  217 us

profile of v2, /device:TPU:40, one launch (start us, length us, event | category | flops | bytes accessed | tf_op | source)
XLA Modules:
  0.0 226.6 jit_solution(17654044410259016166)
XLA Ops:
  0.0 0.7 broadcast_in_dim.29
  0.8 0.7 broadcast_in_dim.30
  1.5 0.7 reduce
  2.2 0.7 copy.39
  2.9 0.1 and_reduce_fusion
  3.0 0.2 copy.34
  3.2 0.1 copy.35
  3.3 0.1 concatenate.9
  3.4 0.1 copy.33
  3.6 0.1 copy.32
  3.7 0.7 min.12.index
  4.4 0.2 copy.36
  4.6 0.6 broadcast_in_dim.33
  5.2 1.4 reshape.70.bias
  6.6 216.8 %shard_map.64 = bf16[512,2048]{1,0:T(8,128)(2,1)} custom-call(s32[2048]{0:T(1024)} %min.12.index, s32[2]{0:T(128)} %bitcast.23, f32[64,8,256]{2,1,0:T(8,128)} %reshape.70.bias, bf16[32,64,512]{2,1,0:T(8,128)(2,1)} %bitcast.15, bf16[32,64,512]{2,1,0:T(8,128)(2,1)} %bitcast.16, bf16[32,64,512]{2,1,0:T(8,128)(2,1)} %bitcast.17, bf16[4,64,2048]{2,1,0:T(8,128)(2,1)} %bitcast.18), custom_call_target="tpu_custom_call" | custom-call | tf_op jit(solution)/shard_map/pallas_call | solution.py:348
  223.5 3.2 %copy.41 = bf16[1,512,2048]{2,1,0:T(8,128)(2,1)} copy(bf16[1,512,2048]{2,1,0:T(8,128)(2,1)} %bitcast.14) | data formatting | bytes 4194304
  (10 shorter events, 0.1 us)

commit v3 on v2

--- a/solution.py
+++ b/solution.py
@@ -16,19 +16,6 @@
 MESH = pl.DeviceIdType.MESH
 
 
-def candidate_blocks(nblocks, glob, rand_h):
-    rows = jnp.arange(nblocks, dtype=jnp.int32)
-    window = jnp.stack([rows - 1, rows, rows + 1], axis=1)
-    globs = jnp.broadcast_to(glob[None, :], (nblocks, glob.shape[0]))
-    cand = jnp.concatenate([window, globs, rand_h], axis=1)
-    inside = (cand >= 0) & (cand < nblocks)
-    width = cand.shape[1]
-    equal = cand[:, :, None] == cand[:, None, :]
-    earlier = jnp.arange(width)[None, :] < jnp.arange(width)[:, None]
-    repeated = jnp.any(equal & earlier[None, :, :], axis=2)
-    return jnp.clip(cand, 0, nblocks - 1), inside & ~repeated
-
-
 def dot(a, b):
     return lax.dot_general(a, b, (((1,), (0,)), ((), ())), preferred_element_type=jnp.float32)
 
@@ -45,9 +32,43 @@
     return jnp.concatenate([x[:, BLK:], x[:, :BLK]], axis=1)
 
 
+def candidates(block, blocks, rand, glob):
+    return [
+        jnp.maximum(block - 1, 0),
+        block,
+        jnp.minimum(block + 1, blocks - 1),
+        glob[0, 0],
+        glob[0, 1],
+    ] + [rand[r, 0, block] for r in range(CAND - 5)]
+
+
+def mark_quad(quad, blocks, bias, rand, glob):
+    at = lane((1, QUAD)) // BLK
+    block = quad * 4 + at
+    cand = [jnp.maximum(block - 1, 0), block, jnp.minimum(block + 1, blocks - 1)]
+    cand += [jnp.full((1, QUAD), glob[0, g], jnp.int32) for g in range(2)]
+    for r in range(CAND - 5):
+        x = [rand[r, 0, quad * 4 + a] for a in range(4)]
+        cand.append(
+            jnp.where(at == 0, x[0], jnp.where(at == 1, x[1], jnp.where(at == 2, x[2], x[3])))
+        )
+    marks = [
+        jnp.where(block == 0, -jnp.inf, 0.0),
+        jnp.zeros((1, QUAD), jnp.float32),
+        jnp.where(block == blocks - 1, -jnp.inf, 0.0),
+    ]
+    for c in range(3, CAND):
+        seen = cand[c] == cand[0]
+        for e in range(1, c):
+            seen = seen | (cand[c] == cand[e])
+        marks.append(jnp.where(seen, -jnp.inf, 0.0))
+    for c in range(CAND):
+        bias[quad, c : c + 1, :] = marks[c].astype(jnp.float32)
+
+
 def take_query(s, q, qg, glob):
     at = lane((HD, LANES))
-    want = jnp.where(at < BLK, glob[0], glob[1])
+    want = jnp.where(at < BLK, glob[0, 0], glob[0, 1])
     kept = qg[...]
     for i in range(q.shape[1] // LANES):
         x = q[:, i * LANES : (i + 1) * LANES]
@@ -109,13 +130,12 @@
     fd[1] = jnp.where(low, other, out)
 
 
-def attend_quad(quad, qq, kd, vd, fd, index, bias, glob):
+def attend_quad(quad, qq, kd, vd, fd, rand, bias, glob):
     low = low_half(BLK)
-    base = quad * (4 * CAND)
     at = lane((HD, QUAD)) // BLK
     zero = jnp.zeros_like(qq)
     weights = jnp.concatenate([jnp.where(at == a, qq, zero) for a in range(4)], axis=0)
-    picks = [[index[base + a * CAND + c] for c in range(CAND)] for a in range(4)]
+    picks = [candidates(quad * 4 + a, kd.shape[0], rand, glob) for a in range(4)]
     keys = []
     for c in range(CAND):
         k = [kd[picks[a][c]] for a in range(4)]
@@ -150,15 +170,8 @@
     here = quad * 4 + at
     for g in range(2):
         f = fd[g]
-        out = jnp.where(here == glob[g], jnp.concatenate([f, f], axis=1), out)
+        out = jnp.where(here == glob[0, g], jnp.concatenate([f, f], axis=1), out)
     return out
-
-
-def tables(glob, rand_h):
-    index, valid = candidate_blocks(rand_h.shape[0], glob, rand_h)
-    marks = jnp.where(valid, 0.0, -jnp.inf).astype(jnp.float32)
-    marks = marks.reshape(-1, 4, CAND).transpose(0, 2, 1)
-    return index.reshape(-1), jnp.repeat(marks, BLK, axis=2)
 
 
 VM = pl.BlockSpec(memory_space=pltpu.VMEM)
@@ -167,22 +180,25 @@
 
 NY = 4
 NZ = 8
-GROUP = 8
-
-
-def offset(i):
+GROUP = 4
+
+
+def offset(i, near):
     a = i // NY
-    dz = NZ // 2 + ((a + 1) // 2) * (1 - 2 * lax.rem(a, 2))
-    return lax.rem(i + 1, NY), dz
-
-
-def target(me, i):
-    dy, dz = offset(i)
+    step = ((a + 1) // 2) * (1 - 2 * lax.rem(a, 2))
+    far = NZ // 2 + step
+    b = lax.rem(a + 1, NZ)
+    close = NZ + ((b + 1) // 2) * (2 * lax.rem(b, 2) - 1)
+    return lax.rem(i + 1, NY), (lax.rem(close, NZ) if near else far)
+
+
+def target(me, i, near):
+    dy, dz = offset(i, near)
     return lax.rem(me // NZ + dy, NY) * NZ + lax.rem(lax.rem(me, NZ) + dz, NZ)
 
 
-def source(me, i):
-    dy, dz = offset(i)
+def source(me, i, near):
+    dy, dz = offset(i, near)
     return lax.rem(me // NZ + NY - dy, NY) * NZ + lax.rem(lax.rem(me, NZ) + NZ - dz, NZ)
 
 
@@ -195,8 +211,8 @@
 
 
 def layer_kernel(
-    index, glob, bias, q, k, v, w, out,
-    qr, kr, vr, kd, vd, fd, qg, held, top, full, ob, att, wr, lhs, total,
+    glob, rand_hbm, q, k, v, w, out,
+    rand, bias, qr, kr, vr, kd, vd, fd, qg, held, top, full, ob, att, wr, lhs, total,
     sent, got, w_sent, w_got, own,
 ):
     devices, _, width = qr.shape
@@ -230,11 +246,11 @@
     pairs = [(q, qr), (k, kr), (v, vr)]
 
     def send(t, i):
-        to = target(me, i)
+        to = target(me, i, True)
         return remote(t, i, pairs[t][0].at[to], pairs[t][1].at[me], to, me)
 
     def arrive(t, i):
-        s = source(me, i)
+        s = source(me, i, True)
         remote(t, i, pairs[t][0].at[s], pairs[t][1].at[s], s, s).wait_recv()
 
     def send_w(i, at):
@@ -249,6 +265,8 @@
         )
 
     copies = [pltpu.make_async_copy(a.at[me], b.at[me], own.at[t]) for t, (a, b) in enumerate(pairs)]
+    table = pltpu.make_async_copy(rand_hbm, rand, own.at[4])
+    table.start()
     copies.append(
         pltpu.make_async_copy(w, wr.at[pl.ds(dp * w.shape[0], w.shape[0])], own.at[3])
     )
@@ -271,67 +289,67 @@
             def _():
                 arrive(t, i)
 
-            f(source(me, i))
+            f(source(me, i, True))
 
         loop(0, devices, one)
 
-    take(0, lambda s: take_query(s, qr.at[s], qg, glob))
+    table.wait()
+
+    def first(s):
+        for h in range(width // QUAD):
+            mark_quad(s * (width // QUAD) + h, kd.shape[0], bias, rand, glob)
+        take_query(s, qr.at[s], qg, glob)
+
+    take(0, first)
     take(1, lambda s: take_key(s, kr.at[s], kd, qg, held, top))
     take(2, lambda s: take_value(s, vr.at[s], vd, held, top, full))
     finish_full(full, fd)
 
     def send_o(i):
-        to = target(me, i)
+        to = target(me, i, False)
         return remote(3, i, ob.at[i], att.at[me], to, me)
 
-    def project(g, last):
-        rows = []
-        heads = [source(me, g * GROUP + j) for j in range(GROUP)]
+    def chunk(i):
+        d = target(me, i, False)
+        for h in range(width // QUAD):
+            cols = slice(h * QUAD, (h + 1) * QUAD)
+            ob[i, :, cols] = attend_quad(
+                d * (width // QUAD) + h, qr[d, :, cols], kd, vd, fd, rand, bias, glob
+            )
+
+        @pl.when(i > 0)
+        def _():
+            send_o(i - 1).start()
+
+    loop(0, devices, chunk)
+    att[me] = ob[devices - 1]
+    copies[3].wait()
+    loop(1, parts, lambda i: send_w(i, lax.rem(dp + parts - i, parts)).wait_recv())
+
+    def project(g, step):
+        heads = [source(me, g * GROUP + j, False) for j in range(GROUP)]
         for j in range(GROUP):
-            s = heads[j]
-            if not (last and j == GROUP - 1):
+            if not (step == 2 and j == GROUP - 1):
+                s = heads[j]
                 remote(3, g * GROUP + j, ob.at[j], att.at[s], s, s).wait_recv()
-            rows.append(att[s])
-        lhs[...] = jnp.concatenate(rows, axis=0).T
+        lhs[...] = jnp.concatenate([att[s] for s in heads], axis=0).T
 
         def tile(n):
             cols = pl.ds(pl.multiple_of(n * QUAD, QUAD), QUAD)
             part = dot(lhs[...], jnp.concatenate([wr[h, :, cols] for h in heads], axis=0))
-            if last:
+            if step == 0:
+                total[:, cols] = part
+            elif step == 1:
+                total[:, cols] += part
+            else:
                 out[:, cols] = (total[:, cols] + part).astype(jnp.bfloat16)
-            else:
-                total[:, cols] += part
 
         loop(0, out.shape[1] // QUAD, tile)
 
-    total[...] = jnp.zeros(total.shape, jnp.float32)
-    copies[3].wait()
-    loop(1, parts, lambda i: send_w(i, lax.rem(dp + parts - i, parts)).wait_recv())
-
-    def group(g):
-        def one(j):
-            i = g * GROUP + j
-            d = target(me, i)
-            for h in range(width // QUAD):
-                cols = slice(h * QUAD, (h + 1) * QUAD)
-                ob[i, :, cols] = attend_quad(
-                    d * (width // QUAD) + h, qr[d, :, cols], kd, vd, fd, index, bias, glob
-                )
-
-            @pl.when(i > 0)
-            def _():
-                send_o(i - 1).start()
-
-        loop(0, GROUP, one)
-
-        @pl.when(g > 0)
-        def _():
-            project(g - 1, False)
-
     groups = devices // GROUP
-    loop(0, groups, group)
-    att[me] = ob[devices - 1]
-    project(groups - 1, True)
+    project(0, 0)
+    loop(1, groups - 1, lambda g: project(g, 1))
+    project(groups - 1, 2)
 
     for t in range(3):
         loop(0, devices - 1, lambda i: send(t, i).wait_send())
@@ -339,7 +357,7 @@
     loop(1, parts, lambda i: send_w(i, dp).wait_send())
 
 
-def layer(index, glob, bias, q, k, v, w, parts):
+def layer(glob, rand, q, k, v, w, parts):
     devices, _, width = q.shape
     blocks = devices * width // BLK
     columns = w.shape[2]
@@ -348,9 +366,11 @@
     return pl.pallas_call(
         layer_kernel,
         out_shape=jax.ShapeDtypeStruct((width, columns), bf),
-        in_specs=[SM, SM, VM, HB, HB, HB, HB],
+        in_specs=[SM, HB, HB, HB, HB, HB],
         out_specs=VM,
         scratch_shapes=[
+            pltpu.SMEM(rand.shape, jnp.int32),
+            pltpu.VMEM((blocks // 4, CAND, QUAD), jnp.float32),
             pltpu.VMEM((devices, HD, width), bf),
             pltpu.VMEM((devices, HD, width), bf),
             pltpu.VMEM((devices, HD, width), bf),
@@ -370,22 +390,20 @@
             dma((4, devices)),
             dma((parts,)),
             dma((parts,)),
-            dma((4,)),
+            dma((5,)),
         ],
         compiler_params=pltpu.CompilerParams(
             collective_id=0, has_side_effects=True, vmem_limit_bytes=60 << 20
         ),
-    )(index, glob, bias, q, k, v, w)
+    )(glob, rand, q, k, v, w)
 
 
 def local(queries, keys, values, random_blocks, global_blocks, out_weight):
-    glob = global_blocks[0]
     width = queries.shape[2]
-    index, bias = tables(glob, random_blocks[0, 0])
     q, k, v = (x[0].reshape(-1, HD, width) for x in (queries, keys, values))
     w = out_weight.reshape(-1, HD, out_weight.shape[1])
     parts = lax.axis_size("dp")
-    return layer(index, glob, bias, q, k, v, w, parts)[None]
+    return layer(global_blocks, random_blocks.transpose(0, 3, 1, 2)[0], q, k, v, w, parts)[None]
 
 
 def solution(mesh):

time: 228 us -> 214 us (0.939)
  Pallas kernels: 217 us -> 211 us
  local copies, waits for them, and re-layouts: 8.87 us -> 3.16 us
    pallas_call x1, Pallas kernels: 217 us -> 211 us  [layer(): pl.pallas_call(layer_kernel, out_shape=jax.ShapeDtypeStruct((width, colum...]
where the time goes in v3:
time: 214 us
  Pallas kernels  211 us (99%)
  local copies, waits for them, and re-layouts  3.16 us (1%)
    pallas_call x1, Pallas kernels, layer(): pl.pallas_call(layer_kernel, out_shape=jax.ShapeDtypeStruct((width, colum...  211 us

profile of v3, /device:TPU:40, one launch (start us, length us, event | category | flops | bytes accessed | tf_op | source)
XLA Modules:
  0.0 214.2 jit_solution(434071005071127085)
XLA Ops:
  0.0 211.0 %shard_map.64 = bf16[512,2048]{1,0:T(8,128)(2,1)} custom-call(s32[1,2]{1,0:T(1,128)} %glob.1, s32[3,1,256]{2,1,0:T(1,128)} %bitcast.13, bf16[32,64,512]{2,1,0:T(8,128)(2,1)} %bitcast.9, bf16[32,64,512]{2,1,0:T(8,128)(2,1)} %bitcast.10, bf16[32,64,512]{2,1,0:T(8,128)(2,1)} %bitcast.11, bf16[4,64,2048]{2,1,0:T(8,128)(2,1)} %bitcast.12), custom_call_target="tpu_custom_call" | custom-call | tf_op jit(solution)/shard_map/pallas_call | solution.py:366
  211.0 3.2 %copy.8 = bf16[1,512,2048]{2,1,0:T(8,128)(2,1)} copy(bf16[1,512,2048]{2,1,0:T(8,128)(2,1)} %bitcast.8) | data formatting | bytes 4194304

commit v4 on v3

--- a/solution.py
+++ b/solution.py
@@ -105,7 +105,11 @@
     return jnp.concatenate([best, best], axis=1)
 
 
-def take_value(s, v, vd, held, top, full):
+def weigh(s, held, best, probs):
+    probs[s] = jnp.exp2(held[s] - best).astype(jnp.bfloat16)
+
+
+def take_value(s, v, vd, probs, full):
     per = v.shape[1] // BLK
     low = low_half(HD)
     for i in range(per // 2):
@@ -114,10 +118,9 @@
         vd[s * per + 2 * i] = jnp.where(low, x, y)
         vd[s * per + 2 * i + 1] = jnp.where(low, y, x)
     half = v.shape[1] // 2
-    probs = jnp.exp2(held[s] - top_of(top)).astype(jnp.bfloat16)
     ones = jnp.ones((16, half), jnp.bfloat16)
     lhs = jnp.concatenate([v[:, :half], v[:, half:], ones], axis=0)
-    full[...] += dot(lhs, probs)
+    full[...] += dot(lhs, probs[s])
 
 
 def finish_full(full, fd):
@@ -176,7 +179,7 @@
 
 VM = pl.BlockSpec(memory_space=pltpu.VMEM)
 SM = pl.BlockSpec(memory_space=pltpu.SMEM)
-HB = pl.BlockSpec(memory_space=pl.ANY)
+HB = pl.BlockSpec(memory_space=pltpu.HBM)
 
 NY = 4
 NZ = 8
@@ -212,7 +215,7 @@
 
 def layer_kernel(
     glob, rand_hbm, q, k, v, w, out,
-    rand, bias, qr, kr, vr, kd, vd, fd, qg, held, top, full, ob, att, wr, lhs, total,
+    rand, bias, qr, kr, vr, kd, vd, fd, qg, held, probs, top, full, ob, att, wr, lhs, total,
     sent, got, w_sent, w_got, own,
 ):
     devices, _, width = qr.shape
@@ -302,7 +305,9 @@
 
     take(0, first)
     take(1, lambda s: take_key(s, kr.at[s], kd, qg, held, top))
-    take(2, lambda s: take_value(s, vr.at[s], vd, held, top, full))
+    best = top_of(top)
+    loop(0, devices, lambda s: weigh(s, held, best, probs))
+    take(2, lambda s: take_value(s, vr.at[s], vd, probs, full))
     finish_full(full, fd)
 
     def send_o(i):
@@ -323,6 +328,8 @@
 
     loop(0, devices, chunk)
     att[me] = ob[devices - 1]
+    for t in range(3):
+        loop(0, devices - 1, lambda i: send(t, i).wait_send())
     copies[3].wait()
     loop(1, parts, lambda i: send_w(i, lax.rem(dp + parts - i, parts)).wait_recv())
 
@@ -351,8 +358,6 @@
     loop(1, groups - 1, lambda g: project(g, 1))
     project(groups - 1, 2)
 
-    for t in range(3):
-        loop(0, devices - 1, lambda i: send(t, i).wait_send())
     loop(0, devices - 1, lambda i: send_o(i).wait_send())
     loop(1, parts, lambda i: send_w(i, dp).wait_send())
 
@@ -365,7 +370,7 @@
     dma = pltpu.SemaphoreType.DMA
     return pl.pallas_call(
         layer_kernel,
-        out_shape=jax.ShapeDtypeStruct((width, columns), bf),
+        out_shape=pltpu.VMEM((width, columns), bf),
         in_specs=[SM, HB, HB, HB, HB, HB],
         out_specs=VM,
         scratch_shapes=[
@@ -379,6 +384,7 @@
             pltpu.VMEM((2, HD, LANES), bf),
             pltpu.VMEM((HD, LANES), bf),
             pltpu.VMEM((devices, width // 2, 2 * LANES), jnp.float32),
+            pltpu.VMEM((devices, width // 2, 2 * LANES), bf),
             pltpu.VMEM((8, 2 * LANES), jnp.float32),
             pltpu.VMEM((2 * HD + 16, 2 * LANES), jnp.float32),
             pltpu.VMEM((devices, HD, width), bf),
@@ -393,7 +399,7 @@
             dma((5,)),
         ],
         compiler_params=pltpu.CompilerParams(
-            collective_id=0, has_side_effects=True, vmem_limit_bytes=60 << 20
+            collective_id=0, has_side_effects=True, vmem_limit_bytes=54 << 20
         ),
     )(glob, rand, q, k, v, w)
 

time: 214 us -> 210 us (0.981)
    pallas_call x1, Pallas kernels: 211 us -> 209 us  [layer(): pl.pallas_call(layer_kernel, out_shape=pltpu.VMEM((width, columns), bf),...]
where the time goes in v4:
time: 210 us
  Pallas kernels  209 us (100%)
    pallas_call x1, Pallas kernels, layer(): pl.pallas_call(layer_kernel, out_shape=pltpu.VMEM((width, columns), bf),...  209 us

profile of v4, /device:TPU:40, one launch (start us, length us, event | category | flops | bytes accessed | tf_op | source)
XLA Modules:
  0.0 210.1 jit_solution(13697510007149275299)
XLA Ops:
  0.0 208.7 %shard_map.64 = bf16[512,2048]{1,0:T(8,128)(2,1)S(1)} custom-call(s32[1,2]{1,0:T(1,128)} %glob.1, s32[3,1,256]{2,1,0:T(1,128)} %bitcast.13, bf16[32,64,512]{2,1,0:T(8,128)(2,1)} %bitcast.9, bf16[32,64,512]{2,1,0:T(8,128)(2,1)} %bitcast.10, bf16[32,64,512]{2,1,0:T(8,128)(2,1)} %bitcast.11, bf16[4,64,2048]{2,1,0:T(8,128)(2,1)} %bitcast.12), custom_call_target="tpu_custom_call" | custom-call | tf_op jit(solution)/shard_map/pallas_call | solution.py:371
  208.7 1.3 copy.8

commit v5 on v4

--- a/solution.py
+++ b/solution.py
@@ -333,10 +333,12 @@
     copies[3].wait()
     loop(1, parts, lambda i: send_w(i, lax.rem(dp + parts - i, parts)).wait_recv())
 
+    groups = devices // GROUP
+
     def project(g, step):
         heads = [source(me, g * GROUP + j, False) for j in range(GROUP)]
         for j in range(GROUP):
-            if not (step == 2 and j == GROUP - 1):
+            if not (not isinstance(g, jax.Array) and g == groups - 1 and j == GROUP - 1):
                 s = heads[j]
                 remote(3, g * GROUP + j, ob.at[j], att.at[s], s, s).wait_recv()
         lhs[...] = jnp.concatenate([att[s] for s in heads], axis=0).T
@@ -353,10 +355,11 @@
 
         loop(0, out.shape[1] // QUAD, tile)
 
-    groups = devices // GROUP
     project(0, 0)
-    loop(1, groups - 1, lambda g: project(g, 1))
-    project(groups - 1, 2)
+    loop(1, 3, lambda g: project(g, 1))
+    project(groups - 1, 1)
+    loop(3, groups - 2, lambda g: project(g, 1))
+    project(groups - 2, 2)
 
     loop(0, devices - 1, lambda i: send_o(i).wait_send())
     loop(1, parts, lambda i: send_w(i, dp).wait_send())

time: 210 us -> 208 us (level)
    pallas_call x1, Pallas kernels: 209 us -> 207 us  [layer(): pl.pallas_call(layer_kernel, out_shape=pltpu.VMEM((width, columns), bf),...]
where the time goes in v5:
time: 208 us
  Pallas kernels  207 us (100%)
    pallas_call x1, Pallas kernels, layer(): pl.pallas_call(layer_kernel, out_shape=pltpu.VMEM((width, columns), bf),...  207 us

profile of v5, /device:TPU:40, one launch (start us, length us, event | category | flops | bytes accessed | tf_op | source)
XLA Modules:
  0.0 207.9 jit_solution(12157949837075059624)
XLA Ops:
  0.0 206.6 %shard_map.64 = bf16[512,2048]{1,0:T(8,128)(2,1)S(1)} custom-call(s32[1,2]{1,0:T(1,128)} %glob.1, s32[3,1,256]{2,1,0:T(1,128)} %bitcast.13, bf16[32,64,512]{2,1,0:T(8,128)(2,1)} %bitcast.9, bf16[32,64,512]{2,1,0:T(8,128)(2,1)} %bitcast.10, bf16[32,64,512]{2,1,0:T(8,128)(2,1)} %bitcast.11, bf16[4,64,2048]{2,1,0:T(8,128)(2,1)} %bitcast.12), custom_call_target="tpu_custom_call" | custom-call | tf_op jit(solution)/shard_map/pallas_call | solution.py:374
  206.6 1.3 copy.8

commit v6 on v5

--- a/solution.py
+++ b/solution.py
@@ -276,7 +276,7 @@
     for t in range(3):
         loop(0, devices - 1, lambda i: send(t, i).start())
         copies[t].start()
-        if t == 0:
+        if t == 2:
             loop(1, parts, lambda i: send_w(i, dp).start())
             copies[3].start()
 

time: 208 us -> 208 us (level)
  no operation moved by 1% of the time
where the time goes in v6:
time: 208 us
  Pallas kernels  207 us (100%)
    pallas_call x1, Pallas kernels, layer(): pl.pallas_call(layer_kernel, out_shape=pltpu.VMEM((width, columns), bf),...  207 us

profile of v6, /device:TPU:40, one launch (start us, length us, event | category | flops | bytes accessed | tf_op | source)
XLA Modules:
  0.0 208.0 jit_solution(15989813306467417182)
XLA Ops:
  0.0 206.7 %shard_map.64 = bf16[512,2048]{1,0:T(8,128)(2,1)S(1)} custom-call(s32[1,2]{1,0:T(1,128)} %glob.1, s32[3,1,256]{2,1,0:T(1,128)} %bitcast.13, bf16[32,64,512]{2,1,0:T(8,128)(2,1)} %bitcast.9, bf16[32,64,512]{2,1,0:T(8,128)(2,1)} %bitcast.10, bf16[32,64,512]{2,1,0:T(8,128)(2,1)} %bitcast.11, bf16[4,64,2048]{2,1,0:T(8,128)(2,1)} %bitcast.12), custom_call_target="tpu_custom_call" | custom-call | tf_op jit(solution)/shard_map/pallas_call | solution.py:374
  206.7 1.3 copy.8
